TPU v7x, 128 devices: a whole 4x4x4 slice. The times are simulated.
128 devices in a mesh: cluster: 8 (over x, core), row: 16 (over z, y).
Axes of the slice: x: 4, y: 4, z: 4, core: 2. Of those that a mesh axis runs over, the one named last changes fastest.
Arguments:
- sources: bfloat16 [32768, 512], P(('cluster', 'row')), may hold values from -12 to 12
- targets: bfloat16 [32768, 512], P(('cluster', 'row')), may hold values from -12 to 12
- source_order: int32 [32768], P(('cluster', 'row')), may hold values from 0 to 255, as said below
- target_order: int32 [32768], P(('cluster', 'row')), may hold values from 0 to 255, as said below
Outputs:
- source_map: bfloat16 [32768, 512], P(('cluster', 'row'))
- target_map: bfloat16 [32768, 512], P(('cluster', 'row'))
Inputs may be any that keep to these rules, and one draw needn't show every extreme that they name: `source_order`: in each aligned block of 256 consecutive rows every value appears exactly once, so each block holds 32 source rows of every co-cluster. `target_order`: in each aligned block of 256 consecutive rows every value appears exactly once, so each block holds 32 target rows of every co-cluster.
All inputs are finite; a program needn't handle non-finite values.
Results may differ from a plain program's by a relative error of at most 0.01.
Values may be sent and summed in bfloat16 or wider, within the bound.
No kernel may reach another device: no remote copies, remote signals or barrier semaphores. Data moves between devices by JAX's collectives and lax.ppermute only.
A program may use at most 64 MiB of HBM per device.

v0:
```python
import math
import jax
import jax.numpy as jnp
from jax import lax
from jax.sharding import PartitionSpec as P

ITERS = 3
entropy_weight = 0.02


def square_sums(matrix):
    widened = matrix.astype(jnp.float32)
    return jnp.sum(widened * widened, axis=1)


def cost_panel(source_rows, source_norms, target_rows, target_norms):
    inner = jnp.einsum("id,jd->ij", source_rows, target_rows, preferred_element_type=jnp.float32)
    return (source_norms[:, None] + target_norms[None, :] - 2.0 * inner) / source_rows.shape[1]


def into_slots(ordering, matrix):
    positions = jnp.arange(matrix.shape[0], dtype=jnp.int32)
    selector = (positions[:, None] == ordering[None, :]).astype(jnp.bfloat16)
    return jnp.dot(selector, matrix, preferred_element_type=jnp.float32).astype(jnp.bfloat16)


def out_of_slots(ordering, matrix):
    positions = jnp.arange(matrix.shape[0], dtype=jnp.int32)
    selector = (ordering[:, None] == positions[None, :]).astype(jnp.bfloat16)
    return jnp.dot(selector, matrix, preferred_element_type=jnp.float32).astype(jnp.bfloat16)


def shards(sources, targets, source_order, target_order):
    rows_dev = sources.shape[0]
    width = sources.shape[1]
    sent_sources = into_slots(source_order, sources)
    sent_targets = into_slots(target_order, targets)
    local_sources, local_targets = (
        lax.all_to_all(sent_sources, "cluster", split_axis=0, concat_axis=0, tiled=True),
        lax.all_to_all(sent_targets, "cluster", split_axis=0, concat_axis=0, tiled=True),
    )
    cluster_targets = lax.all_gather(local_targets, "row", axis=0, tiled=True)
    columns = cluster_targets.shape[0]
    span = 512
    pieces = columns // span
    target_norms = square_sums(cluster_targets)
    target_blocks = cluster_targets.reshape(pieces, span, width)
    norm_blocks = target_norms.reshape(pieces, span)
    source_norms = square_sums(local_sources)
    log_mass = -math.log(columns)

    def row_lse(potential):

        def row_advance(carry, item):
            running, totals = carry
            block, block_norms, block_potential = item
            scores = (
                block_potential[None, :]
                - cost_panel(local_sources, source_norms, block, block_norms)
            ) / entropy_weight
            highest = jnp.maximum(running, jnp.max(scores, axis=1))
            totals = totals * jnp.exp(running - highest) + jnp.sum(
                jnp.exp(scores - highest[:, None]), axis=1
            )
            return ((highest, totals), None)

        start = (jnp.full((rows_dev,), -jnp.inf, jnp.float32), jnp.zeros((rows_dev,), jnp.float32))
        (running, totals), unused = lax.scan(
            row_advance, start, (target_blocks, norm_blocks, potential.reshape(pieces, span))
        )
        return running + jnp.log(totals)

    def column_lse(source_potential):

        def column_advance(carry, item):
            block, block_norms = item
            scores = (
                source_potential[:, None]
                - cost_panel(local_sources, source_norms, block, block_norms)
            ) / entropy_weight
            highest = jnp.max(scores, axis=0)
            return (carry, (highest, jnp.sum(jnp.exp(scores - highest[None, :]), axis=0)))

        unused, (peaks, totals) = lax.scan(column_advance, 0, (target_blocks, norm_blocks))
        peaks = peaks.reshape(-1)
        totals = totals.reshape(-1)
        highest = lax.pmax(peaks, "row")
        summed = lax.psum(totals * jnp.exp(peaks - highest), "row")
        return highest + jnp.log(summed)

    target_potential = jnp.zeros((columns,), jnp.float32)
    for repeat in range(ITERS):
        source_potential = entropy_weight * (log_mass - row_lse(target_potential))
        column_norm = column_lse(source_potential)
        target_potential = entropy_weight * (log_mass - column_norm)
    block = cluster_targets
    block_norms = target_norms
    scores = (
        source_potential[:, None] - cost_panel(local_sources, source_norms, block, block_norms)
    ) / entropy_weight
    weights = jnp.exp(scores - column_norm[None, :]).astype(jnp.bfloat16)
    target_map = lax.psum_scatter(
        jnp.einsum("ij,id->jd", weights, local_sources, preferred_element_type=jnp.float32).astype(
            jnp.bfloat16
        ),
        "row",
        scatter_dimension=0,
        tiled=True,
    )
    row_norm = row_lse(target_potential)

    def accumulate(carry, item):
        block, block_norms, block_potential = item
        scores = (
            block_potential[None, :] - cost_panel(local_sources, source_norms, block, block_norms)
        ) / entropy_weight
        weights = jnp.exp(scores - row_norm[:, None]).astype(jnp.bfloat16)
        return (carry + jnp.dot(weights, block, preferred_element_type=jnp.float32), None)

    source_sums, unused = lax.scan(
        accumulate,
        jnp.zeros((rows_dev, width), jnp.float32),
        (target_blocks, norm_blocks, target_potential.reshape(pieces, span)),
    )
    source_map = source_sums.astype(jnp.bfloat16)
    back_sources, back_targets = (
        lax.all_to_all(source_map, "cluster", split_axis=0, concat_axis=0, tiled=True),
        lax.all_to_all(target_map, "cluster", split_axis=0, concat_axis=0, tiled=True),
    )
    return (out_of_slots(source_order, back_sources), out_of_slots(target_order, back_targets))


def solution(mesh):
    return jax.shard_map(
        shards,
        mesh=mesh,
        in_specs=(
            P(("cluster", "row"), None),
            P(("cluster", "row"), None),
            P(("cluster", "row")),
            P(("cluster", "row")),
        ),
        out_specs=(P(("cluster", "row"), None), P(("cluster", "row"), None)),
        check_vma=False,
    )
```

profile of v0, /device:TPU:1, one launch (start us, length us, event | category | flops | bytes accessed | tf_op | source)
XLA Modules:
  0.0 678.2 jit_solution(1268138748987792291)
XLA Ops:
  9.0 12.2 %all_to_all.48 = bf16[8,32,512]{2,1,0:T(8,128)(2,1)} all-to-all(bf16[8,32,512]{2,1,0:T(8,128)(2,1)S(1)} %bitcast.260), channel_id=1, replica_groups=mesh['cluster'=8,'row'=16] {'cluster'}, dimensions={0} | all-to-all | bytes 524288 | tf_op jit(solution)/shard_map/all_to_all | solution.py:40
  23.1 4.4 all-to-all-start
  27.6 6.4 all-to-all-done
  34.2 39.4 %all-gather.2.cloned.1.call-done = bf16[4096,512]{1,0:T(8,128)(2,1)} async-done(((bf16[256,512]{1,0:T(8,128)(2,1)}), bf16[4096,512]{1,0:T(8,128)(2,1)}) %all-gather.2.cloned.1.call-update) | async-done | bytes 4194320 | tf_op jit(solution)/shard_map/all_gather | solution.py:42
  73.6 3.1 multiply_reduce_fusion
  76.7 12.7 %while.102 = (s32[]{:T(128)}, f32[256]{0:T(256)S(1)}, f32[256]{0:T(256)S(1)}, f32[256]{0:T(256)S(1)}, f32[8,512]{1,0:T(8,128)S(1)}, /*index=5*/bf16[8,512,512]{2...) while((s32[]{:T(128)}, f32[256]{0:T(256)S(1)}, f32[256]{0:T(256)S(1)}, ...), condition=%wide.region_5.6_spmd.clone, body=%wide.region_2.5_spmd.clone.sunk | while | flops 135398656 | bytes 1856108 | solution.py:68
  89.5 13.7 %while.99 = (s32[]{:T(128)}, f32[8,512]{1,0:T(8,128)S(1)}, f32[8,512]{1,0:T(8,128)S(1)}, f32[256]{0:T(256)S(1)}, f32[256]{0:T(256)S(1)}, /*index=5*/f32[8,512]{1...) while((s32[]{:T(128)}, f32[8,512]{1,0:T(8,128)S(1)}, ...), condition=%wide.region_9.10_spmd, body=%wide.region_6.9_spmd.sunk | while | flops 135396352 | bytes 1858161 | solution.py:84
  103.2 58.3 %pmax.21 = f32[4096]{0:T(1024)S(1)} all-reduce(f32[4096]{0:T(1024)S(1)} %bitcast.268), channel_id=1, replica_groups=mesh['cluster'=8,'row'=16] {'row'}, use_global_device_ids=true, to_apply=%region_10.11 | all-reduce | flops 4096 | bytes 32768 | tf_op jit(solution)/shard_map/pmax | solution.py:87
  161.5 55.6 %psum.21 = f32[4096]{0:T(1024)S(1)} all-reduce(f32[4096]{0:T(1024)S(1)} %exponential_multiply_fusion.2), channel_id=1, replica_groups=mesh['cluster'=8,'row'=16] {'row'}, use_global_device_ids=true, to_apply=%region_11.12 | all-reduce | flops 4096 | bytes 32768 | tf_op jit(solution)/shard_map/psum | solution.py:88
  217.1 12.8 %while.103 = (s32[]{:T(128)}, f32[256]{0:T(256)S(1)}, f32[256]{0:T(256)S(1)}, f32[8,512]{1,0:T(8,128)S(1)}, f32[256]{0:T(256)S(1)}, /*index=5*/f32[8,512]{1,0:T(...) while((s32[]{:T(128)}, f32[256]{0:T(256)S(1)}, ...), condition=%wide.region_15.16_spmd.clone, body=%wide.region_12.15_spmd.clone.sunk | while | flops 135398656 | bytes 1862260 | solution.py:68
  230.0 13.7 %while.100 = (s32[]{:T(128)}, f32[8,512]{1,0:T(8,128)S(1)}, f32[8,512]{1,0:T(8,128)S(1)}, f32[256]{0:T(256)S(1)}, f32[256]{0:T(256)S(1)}, /*index=5*/f32[8,512]{...) while((s32[]{:T(128)}, f32[8,512]{1,0:T(8,128)S(1)}, ...), condition=%wide.region_19.20_spmd, body=%wide.region_16.19_spmd.sunk | while | flops 135396352 | bytes 1858161 | solution.py:84
  243.7 55.6 %pmax.22 = f32[4096]{0:T(1024)S(1)} all-reduce(f32[4096]{0:T(1024)S(1)} %bitcast.270), channel_id=1, replica_groups=mesh['cluster'=8,'row'=16] {'row'}, use_global_device_ids=true, to_apply=%region_20.21 | all-reduce | flops 4096 | bytes 32768 | tf_op jit(solution)/shard_map/pmax | solution.py:87
  299.4 56.0 %psum.22 = f32[4096]{0:T(1024)S(1)} all-reduce(f32[4096]{0:T(1024)S(1)} %exponential_multiply_fusion.1), channel_id=1, replica_groups=mesh['cluster'=8,'row'=16] {'row'}, use_global_device_ids=true, to_apply=%region_21.22 | all-reduce | flops 4096 | bytes 32768 | tf_op jit(solution)/shard_map/psum | solution.py:88
  355.3 12.8 %while.104 = (s32[]{:T(128)}, f32[256]{0:T(256)S(1)}, f32[256]{0:T(256)S(1)}, f32[8,512]{1,0:T(8,128)S(1)}, f32[256]{0:T(256)S(1)}, /*index=5*/f32[8,512]{1,0:T(...) while((s32[]{:T(128)}, f32[256]{0:T(256)S(1)}, ...), condition=%wide.region_25.26_spmd.clone, body=%wide.region_22.25_spmd.clone.sunk | while | flops 135398656 | bytes 1862260 | solution.py:68
  368.2 13.7 %while.101 = (s32[]{:T(128)}, f32[8,512]{1,0:T(8,128)S(1)}, f32[8,512]{1,0:T(8,128)S(1)}, f32[256]{0:T(256)S(1)}, f32[256]{0:T(256)S(1)}, /*index=5*/f32[8,512]{...) while((s32[]{:T(128)}, f32[8,512]{1,0:T(8,128)S(1)}, ...), condition=%wide.region_29.30_spmd, body=%wide.region_26.29_spmd.sunk | while | flops 135396352 | bytes 1858161 | solution.py:84
  382.0 55.6 %pmax.23 = f32[4096]{0:T(1024)S(1)} all-reduce(f32[4096]{0:T(1024)S(1)} %bitcast.272), channel_id=1, replica_groups=mesh['cluster'=8,'row'=16] {'row'}, use_global_device_ids=true, to_apply=%region_30.31 | all-reduce | flops 4096 | bytes 32768 | tf_op jit(solution)/shard_map/pmax | solution.py:87
  437.6 55.6 %psum.23 = f32[4096]{0:T(1024)S(1)} all-reduce(f32[4096]{0:T(1024)S(1)} %exponential_multiply_fusion), channel_id=1, replica_groups=mesh['cluster'=8,'row'=16] {'row'}, use_global_device_ids=true, to_apply=%region_31.32 | all-reduce | flops 4096 | bytes 32768 | tf_op jit(solution)/shard_map/psum | solution.py:88
  493.2 7.0 %convolution_convert_fusion = bf16[4096,512]{1,0:T(8,128)(2,1)} fusion(bf16[256,512]{1,0:T(8,128)(2,1)S(1)} %get-tuple-element.1322, bf16[4096,512]{1,0:T(8,128)(2,1)} %bitcast.254, f32[4096]{0:T(1024)S(1)} %get-tuple-element.614, f32[4096]{0:T(1024)S(1)} %multiply_reduce_fusion, f32[256]{0:T(256)S(1)} %get-tuple-element.1343, f32[256]{0:T(256)S(1)} %get-tuple-element.1345), kind=kOutput, calls=%fused_computation.123 | convolution fusion | flops 2157969408 | bytes 8685568 | tf_op jit(solution)/shard_map/ij,id->jd/dot_general | solution.py:103
  500.2 12.8 %while.105 = (s32[]{:T(128)}, f32[256]{0:T(256)S(1)}, f32[256]{0:T(256)S(1)}, f32[8,512]{1,0:T(8,128)S(1)}, f32[256]{0:T(256)S(1)}, /*index=5*/f32[8,512]{1,0:T(...) while((s32[]{:T(128)}, f32[256]{0:T(256)S(1)}, ...), condition=%wide.region_35.36_spmd.clone, body=%wide.region_32.35_spmd.clone.sunk | while | flops 135398656 | bytes 1862260 | solution.py:68
  513.1 15.4 %while.106 = (s32[]{:T(128)}, f32[256,512]{1,0:T(8,128)S(1)}, f32[8,512]{1,0:T(8,128)S(1)}, f32[256]{0:T(256)S(1)}, f32[8,512]{1,0:T(8,128)S(1)}, /*index=5*/bf1...) while((s32[]{:T(128)}, f32[256,512]{1,0:T(8,128)S(1)}, ...), condition=%wide.region_37.38_spmd.clone, body=%wide.region_36.37_spmd.clone.sunk | while | flops 269746176 | bytes 2374771 | solution.py:120
  528.5 94.9 %all_to_all.49 = bf16[8,32,512]{2,1,0:T(8,128)(2,1)S(1)} all-to-all(bf16[8,32,512]{2,1,0:T(8,128)(2,1)S(1)} %bitcast.255), channel_id=1, replica_groups=mesh['cluster'=8,'row'=16] {'cluster'}, dimensions={0} | all-to-all | bytes 524288 | tf_op jit(solution)/shard_map/all_to_all | solution.py:127
  623.4 33.8 %reduce-scatter.2.cloned.1.call-done = bf16[256,512]{1,0:T(8,128)(2,1)} async-done(((bf16[4096,512]{1,0:T(8,128)(2,1)}), bf16[256,512]{1,0:T(8,128)(2,1)}) %reduce-scatter.2.cloned.1.call-update) | async-done | bytes 262160 | tf_op jit(solution)/shard_map/reduce_scatter | solution.py:102
  657.2 6.7 all-to-all-start.3
  664.9 5.5 all-to-all-done.3
  (380 shorter events, 111.3 us)
Async XLA Ops:
  7.2 1.0 copy-start
  7.2 66.4 %all-gather.2.cloned.1.call-start = ((), (), s32[]{:S(2)}) async-start(), calls=%async_computation.5 | async-start | bytes 4456448 | tf_op jit(solution)/shard_map/all_gather | solution.py:42
  23.1 10.8 %all-to-all-start = ((bf16[8,32,512]{2,1,0:T(8,128)(2,1)}), bf16[8,32,512]{2,1,0:T(8,128)(2,1)S(1)}, u32[]{:S(2)}, u32[]{:S(2)}) async-start(bf16[8,32,512]{2,1,0:T(8,128)(2,1)} %bitcast.15), calls=%async_computation | async-start | bytes 524288 | tf_op jit(solution)/shard_map/all_to_all | solution.py:39
  27.5 629.7 %reduce-scatter.2.cloned.1.call-start = ((), (), s32[]{:S(2)}) async-start(), calls=%async_computation.6 | async-start | bytes 4456448 | tf_op jit(solution)/shard_map/reduce_scatter | solution.py:102
  513.1 150.8 %copy-start.1 = (s32[256]{0:T(256)S(1)}, s32[256]{0:T(256)}, u32[]{:S(2)}) copy-start(s32[256]{0:T(256)} %param.22) | copy-start | bytes 3076
  513.1 157.3 %copy-start.2 = (s32[256]{0:T(256)S(1)}, s32[256]{0:T(256)}, u32[]{:S(2)}) copy-start(s32[256]{0:T(256)} %param.23) | copy-start | bytes 3076
  657.2 13.2 %all-to-all-start.3 = ((bf16[8,32,512]{2,1,0:T(8,128)(2,1)}), bf16[8,32,512]{2,1,0:T(8,128)(2,1)S(1)}, u32[]{:S(2)}, u32[]{:S(2)}) async-start(bf16[8,32,512]{2,1,0:T(8,128)(2,1)} %bitcast.261), calls=%async_computation.4 | async-start | bytes 524288 | tf_op jit(solution)/shard_map/all_to_all | solution.py:128
Sparse Core Ops, SparseCore 0:
  21.3 52.2 all-gather.1
  500.3 156.7 reduce-scatter.1
where the time goes:
time: 682 us; the launch traced here: 678 us
  blocking collectives  444 us (65%)
  matrix products  106 us (16%)
  waiting for transfers between devices  85.2 us (12%)
  between operations  14.3 us (2%)
  starting transfers between devices  11.1 us (2%)
  other arithmetic  10.7 us (2%)
    pmax x3, blocking collectives, column_lse(): highest = lax.pmax(peaks, 'row')  170 us
    psum x3, blocking collectives, column_lse(): summed = lax.psum(totals * jnp.exp(peaks - highest), 'row')  167 us
    all_to_all x1, blocking collectives, shards(): lax.all_to_all(source_map, 'cluster', split_axis=0, concat_axis=0, tiled=...  94.9 us
    dot_general x56, matrix products, cost_panel(): jnp.einsum('id,jd->ij', source_rows, target_rows, preferred_element_type=...  79.3 us
    all_gather x1, waiting for transfers between devices, shards(): cluster_targets = lax.all_gather(local_targets, 'row', axis=0, tiled=True)  39.4 us
    reduce_scatter x1, waiting for transfers between devices, shards(): lax.psum_scatter(jnp.einsum('ij,id->jd', weights, local_sources, preferre...  33.8 us
    dot_general x8, matrix products, accumulate(): jnp.dot(weights, block, preferred_element_type=jnp.float32)  15 us
  transfers between devices with their start and end apart: 4, of which 4 were waited for; matrix products, arithmetic and copies ran while one was open for 5% of the time, Pallas kernels for 0%

commit v1 on v0

--- a/solution.py
+++ b/solution.py
@@ -6,6 +6,29 @@
 
 ITERS = 3
 entropy_weight = 0.02
+
+
+def in_blocks(shard, dim, size):
+    lengths = shard.shape
+    pieces = shard.reshape(*lengths[:dim], size, lengths[dim] // size, *lengths[dim + 1 :])
+    return jnp.moveaxis(pieces, dim, 0)
+
+
+def in_order(tiles, dim):
+    dims = list(tiles.shape[1:])
+    dims[dim] *= tiles.shape[0]
+    return jnp.moveaxis(tiles, 0, dim).reshape(dims)
+
+
+def exchange_in_pairs(x, axis, split_dim, concat_dim):
+    size, index = (lax.axis_size(axis), lax.axis_index(axis))
+    parts = in_blocks(x, split_dim, size)
+    done = [parts[index]]
+    for lap in range(1, size):
+        sent = parts[index ^ lap]
+        done.append(lax.ppermute(sent, axis, [(i, i ^ lap) for i in range(size)]))
+    parts = jnp.stack(done)[index ^ jnp.arange(size)]
+    return in_order(parts, concat_dim)
 
 
 def square_sums(matrix):
@@ -124,7 +147,7 @@
     )
     source_map = source_sums.astype(jnp.bfloat16)
     back_sources, back_targets = (
-        lax.all_to_all(source_map, "cluster", split_axis=0, concat_axis=0, tiled=True),
+        exchange_in_pairs(source_map, "cluster", 0, 0),
         lax.all_to_all(target_map, "cluster", split_axis=0, concat_axis=0, tiled=True),
     )
     return (out_of_slots(source_order, back_sources), out_of_slots(target_order, back_targets))

time: 682 us -> 682 us (level)
  blocking collectives: 444 us -> 349 us
  starting transfers between devices: 11.1 us -> 104 us
    all_to_all x1 -> x0, blocking collectives: 94.9 us -> none  [shards(): lax.all_to_all(source_map, 'cluster', split_axis=0, concat_axis=0, tiled=...]
    ppermute x0 -> x7, starting transfers between devices: none -> 92.4 us  [exchange_in_pairs(): done.append(lax.ppermute(sent, axis, [(i, i ^ lap) for i in range(size)]))]
  transfers between devices with their start and end apart: 4 -> 11, of which waited for: 4 -> 7; matrix products, arithmetic and copies ran while one was open for 5% -> 5% of each run, Pallas kernels for 0% -> 0%
where the time goes in v1:
time: 682 us; the launch traced here: 678 us
  blocking collectives  349 us (51%)
  matrix products  106 us (16%)
  starting transfers between devices  104 us (15%)
  waiting for transfers between devices  86.9 us (13%)
  between operations  14.4 us (2%)
  other arithmetic  10.8 us (2%)
    pmax x3, blocking collectives, column_lse(): highest = lax.pmax(peaks, 'row')  170 us
    psum x3, blocking collectives, column_lse(): summed = lax.psum(totals * jnp.exp(peaks - highest), 'row')  167 us
    ppermute x7, starting transfers between devices, exchange_in_pairs(): done.append(lax.ppermute(sent, axis, [(i, i ^ lap) for i in range(size)]))  92.4 us
    dot_general x56, matrix products, cost_panel(): jnp.einsum('id,jd->ij', source_rows, target_rows, preferred_element_type=...  79.3 us
    all_gather x1, waiting for transfers between devices, shards(): cluster_targets = lax.all_gather(local_targets, 'row', axis=0, tiled=True)  39.4 us
    reduce_scatter x1, waiting for transfers between devices, shards(): lax.psum_scatter(jnp.einsum('ij,id->jd', weights, local_sources, preferre...  31.3 us
    dot_general x8, matrix products, accumulate(): jnp.dot(weights, block, preferred_element_type=jnp.float32)  15 us
  transfers between devices with their start and end apart: 11, of which 7 were waited for; matrix products, arithmetic and copies ran while one was open for 5% of the time, Pallas kernels for 0%

profile of v1, /device:TPU:1, one launch (start us, length us, event | category | flops | bytes accessed | tf_op | source)
XLA Modules:
  0.0 678.2 jit_solution(10181776148048518780)
XLA Ops:
  9.0 12.2 %all_to_all.36 = bf16[8,32,512]{2,1,0:T(8,128)(2,1)} all-to-all(bf16[8,32,512]{2,1,0:T(8,128)(2,1)S(1)} %bitcast.290), channel_id=1, replica_groups=mesh['cluster'=8,'row'=16] {'cluster'}, dimensions={0} | all-to-all | bytes 524288 | tf_op jit(solution)/shard_map/all_to_all | solution.py:63
  23.1 4.4 all-to-all-start
  27.6 6.4 all-to-all-done
  34.2 39.4 %all-gather.2.cloned.1.call-done = bf16[4096,512]{1,0:T(8,128)(2,1)} async-done(((bf16[256,512]{1,0:T(8,128)(2,1)}), bf16[4096,512]{1,0:T(8,128)(2,1)}) %all-gather.2.cloned.1.call-update) | async-done | bytes 4194320 | tf_op jit(solution)/shard_map/all_gather | solution.py:65
  73.6 3.1 multiply_reduce_fusion
  76.7 12.7 %while.102 = (s32[]{:T(128)}, f32[256]{0:T(256)S(1)}, f32[256]{0:T(256)S(1)}, f32[256]{0:T(256)S(1)}, f32[8,512]{1,0:T(8,128)S(1)}, /*index=5*/bf16[8,512,512]{2...) while((s32[]{:T(128)}, f32[256]{0:T(256)S(1)}, f32[256]{0:T(256)S(1)}, ...), condition=%wide.region_5.6_spmd.clone, body=%wide.region_2.5_spmd.clone.sunk | while | flops 135398656 | bytes 1856108 | solution.py:91
  89.5 13.7 %while.99 = (s32[]{:T(128)}, f32[8,512]{1,0:T(8,128)S(1)}, f32[8,512]{1,0:T(8,128)S(1)}, f32[256]{0:T(256)S(1)}, f32[256]{0:T(256)S(1)}, /*index=5*/f32[8,512]{1...) while((s32[]{:T(128)}, f32[8,512]{1,0:T(8,128)S(1)}, ...), condition=%wide.region_9.10_spmd, body=%wide.region_6.9_spmd.sunk | while | flops 135396352 | bytes 1858161 | solution.py:107
  103.2 58.3 %pmax.21 = f32[4096]{0:T(1024)S(1)} all-reduce(f32[4096]{0:T(1024)S(1)} %bitcast.298), channel_id=1, replica_groups=mesh['cluster'=8,'row'=16] {'row'}, use_global_device_ids=true, to_apply=%region_10.11 | all-reduce | flops 4096 | bytes 32768 | tf_op jit(solution)/shard_map/pmax | solution.py:110
  161.5 55.6 %psum.21 = f32[4096]{0:T(1024)S(1)} all-reduce(f32[4096]{0:T(1024)S(1)} %exponential_multiply_fusion.2), channel_id=1, replica_groups=mesh['cluster'=8,'row'=16] {'row'}, use_global_device_ids=true, to_apply=%region_11.12 | all-reduce | flops 4096 | bytes 32768 | tf_op jit(solution)/shard_map/psum | solution.py:111
  217.1 12.8 %while.103 = (s32[]{:T(128)}, f32[256]{0:T(256)S(1)}, f32[256]{0:T(256)S(1)}, f32[8,512]{1,0:T(8,128)S(1)}, f32[256]{0:T(256)S(1)}, /*index=5*/f32[8,512]{1,0:T(...) while((s32[]{:T(128)}, f32[256]{0:T(256)S(1)}, ...), condition=%wide.region_15.16_spmd.clone, body=%wide.region_12.15_spmd.clone.sunk | while | flops 135398656 | bytes 1862260 | solution.py:91
  230.0 13.7 %while.100 = (s32[]{:T(128)}, f32[8,512]{1,0:T(8,128)S(1)}, f32[8,512]{1,0:T(8,128)S(1)}, f32[256]{0:T(256)S(1)}, f32[256]{0:T(256)S(1)}, /*index=5*/f32[8,512]{...) while((s32[]{:T(128)}, f32[8,512]{1,0:T(8,128)S(1)}, ...), condition=%wide.region_19.20_spmd, body=%wide.region_16.19_spmd.sunk | while | flops 135396352 | bytes 1858161 | solution.py:107
  243.7 55.6 %pmax.22 = f32[4096]{0:T(1024)S(1)} all-reduce(f32[4096]{0:T(1024)S(1)} %bitcast.300), channel_id=1, replica_groups=mesh['cluster'=8,'row'=16] {'row'}, use_global_device_ids=true, to_apply=%region_20.21 | all-reduce | flops 4096 | bytes 32768 | tf_op jit(solution)/shard_map/pmax | solution.py:110
  299.4 56.0 %psum.22 = f32[4096]{0:T(1024)S(1)} all-reduce(f32[4096]{0:T(1024)S(1)} %exponential_multiply_fusion.1), channel_id=1, replica_groups=mesh['cluster'=8,'row'=16] {'row'}, use_global_device_ids=true, to_apply=%region_21.22 | all-reduce | flops 4096 | bytes 32768 | tf_op jit(solution)/shard_map/psum | solution.py:111
  355.3 12.8 %while.104 = (s32[]{:T(128)}, f32[256]{0:T(256)S(1)}, f32[256]{0:T(256)S(1)}, f32[8,512]{1,0:T(8,128)S(1)}, f32[256]{0:T(256)S(1)}, /*index=5*/f32[8,512]{1,0:T(...) while((s32[]{:T(128)}, f32[256]{0:T(256)S(1)}, ...), condition=%wide.region_25.26_spmd.clone, body=%wide.region_22.25_spmd.clone.sunk | while | flops 135398656 | bytes 1862260 | solution.py:91
  368.2 13.7 %while.101 = (s32[]{:T(128)}, f32[8,512]{1,0:T(8,128)S(1)}, f32[8,512]{1,0:T(8,128)S(1)}, f32[256]{0:T(256)S(1)}, f32[256]{0:T(256)S(1)}, /*index=5*/f32[8,512]{...) while((s32[]{:T(128)}, f32[8,512]{1,0:T(8,128)S(1)}, ...), condition=%wide.region_29.30_spmd, body=%wide.region_26.29_spmd.sunk | while | flops 135396352 | bytes 1858161 | solution.py:107
  382.0 55.6 %pmax.23 = f32[4096]{0:T(1024)S(1)} all-reduce(f32[4096]{0:T(1024)S(1)} %bitcast.302), channel_id=1, replica_groups=mesh['cluster'=8,'row'=16] {'row'}, use_global_device_ids=true, to_apply=%region_30.31 | all-reduce | flops 4096 | bytes 32768 | tf_op jit(solution)/shard_map/pmax | solution.py:110
  437.6 55.6 %psum.23 = f32[4096]{0:T(1024)S(1)} all-reduce(f32[4096]{0:T(1024)S(1)} %exponential_multiply_fusion), channel_id=1, replica_groups=mesh['cluster'=8,'row'=16] {'row'}, use_global_device_ids=true, to_apply=%region_31.32 | all-reduce | flops 4096 | bytes 32768 | tf_op jit(solution)/shard_map/psum | solution.py:111
  493.2 7.0 %convolution_convert_fusion = bf16[4096,512]{1,0:T(8,128)(2,1)} fusion(bf16[256,512]{1,0:T(8,128)(2,1)S(1)} %get-tuple-element.1330, bf16[4096,512]{1,0:T(8,128)(2,1)} %bitcast.284, f32[4096]{0:T(1024)S(1)} %get-tuple-element.614, f32[4096]{0:T(1024)S(1)} %multiply_reduce_fusion, f32[256]{0:T(256)S(1)} %get-tuple-element.1365, f32[256]{0:T(256)S(1)} %get-tuple-element.1367), kind=kOutput, calls=%fused_computation.124 | convolution fusion | flops 2157969408 | bytes 8685568 | tf_op jit(solution)/shard_map/ij,id->jd/dot_general | solution.py:126
  500.2 12.8 %while.105 = (s32[]{:T(128)}, f32[256]{0:T(256)S(1)}, f32[256]{0:T(256)S(1)}, f32[8,512]{1,0:T(8,128)S(1)}, f32[256]{0:T(256)S(1)}, /*index=5*/f32[8,512]{1,0:T(...) while((s32[]{:T(128)}, f32[256]{0:T(256)S(1)}, ...), condition=%wide.region_35.36_spmd.clone, body=%wide.region_32.35_spmd.clone.sunk | while | flops 135398656 | bytes 1862260 | solution.py:91
  513.1 15.4 %while.106 = (s32[]{:T(128)}, f32[256,512]{1,0:T(8,128)S(1)}, f32[8,512]{1,0:T(8,128)S(1)}, f32[256]{0:T(256)S(1)}, f32[8,512]{1,0:T(8,128)S(1)}, /*index=5*/bf1...) while((s32[]{:T(128)}, f32[256,512]{1,0:T(8,128)S(1)}, ...), condition=%wide.region_37.38_spmd.clone, body=%wide.region_36.37_spmd.clone.sunk | while | flops 269746176 | bytes 2374771 | solution.py:143
  528.6 84.5 %collective-permute-start = (bf16[32,512]{1,0:T(8,128)(2,1)S(1)}, bf16[32,512]{1,0:T(8,128)(2,1)S(1)}, u32[]{:S(2)}, u32[]{:S(2)}) collective-permute-start(bf16[32,512]{1,0:T(8,128)(2,1)S(1)} %get-tuple-element.643), channel_id=1, source_target_pairs={{0,16},{16,0},{32,48},{48,32},{64,80},{80,64},{96,112},{112,96},{1... | collective-permute-start | bytes 98312 | tf_op jit(solution)/shard_map/ppermute | solution.py:29
  625.8 31.3 %reduce-scatter.2.cloned.1.call-done = bf16[256,512]{1,0:T(8,128)(2,1)} async-done(((bf16[4096,512]{1,0:T(8,128)(2,1)}), bf16[256,512]{1,0:T(8,128)(2,1)}) %reduce-scatter.2.cloned.1.call-update) | async-done | bytes 262160 | tf_op jit(solution)/shard_map/reduce_scatter | solution.py:125
  657.2 6.7 all-to-all-start.2
  664.9 5.5 all-to-all-done.2
  (404 shorter events, 124.1 us)
Async XLA Ops:
  7.2 1.0 copy-start
  7.2 66.4 %all-gather.2.cloned.1.call-start = ((), (), s32[]{:S(2)}) async-start(), calls=%async_computation.4 | async-start | bytes 4456448 | tf_op jit(solution)/shard_map/all_gather | solution.py:65
  23.1 10.8 %all-to-all-start = ((bf16[8,32,512]{2,1,0:T(8,128)(2,1)}), bf16[8,32,512]{2,1,0:T(8,128)(2,1)S(1)}, u32[]{:S(2)}, u32[]{:S(2)}) async-start(bf16[8,32,512]{2,1,0:T(8,128)(2,1)} %bitcast.15), calls=%async_computation | async-start | bytes 524288 | tf_op jit(solution)/shard_map/all_to_all | solution.py:62
  27.5 629.7 %reduce-scatter.2.cloned.1.call-start = ((), (), s32[]{:S(2)}) async-start(), calls=%async_computation.5 | async-start | bytes 4456448 | tf_op jit(solution)/shard_map/reduce_scatter | solution.py:125
  513.1 150.8 %copy-start.1 = (s32[256]{0:T(256)S(1)}, s32[256]{0:T(256)}, u32[]{:S(2)}) copy-start(s32[256]{0:T(256)} %param.22) | copy-start | bytes 3076
  513.1 157.3 %copy-start.2 = (s32[256]{0:T(256)S(1)}, s32[256]{0:T(256)}, u32[]{:S(2)}) copy-start(s32[256]{0:T(256)} %param.23) | copy-start | bytes 3076
  528.6 89.5 %collective-permute-start = (bf16[32,512]{1,0:T(8,128)(2,1)S(1)}, bf16[32,512]{1,0:T(8,128)(2,1)S(1)}, u32[]{:S(2)}, u32[]{:S(2)}) collective-permute-start(bf16[32,512]{1,0:T(8,128)(2,1)S(1)} %get-tuple-element.643), channel_id=1, source_target_pairs={{0,16},{16,0},{32,48},{48,32},{64,80},{80,64},{96,112},{112,96},{1... | collective-permute-start | bytes 98312 | tf_op jit(solution)/shard_map/ppermute | solution.py:29
  613.1 7.3 %collective-permute-start.1 = (bf16[32,512]{1,0:T(8,128)(2,1)S(1)}, bf16[32,512]{1,0:T(8,128)(2,1)S(1)}, u32[]{:S(2)}, u32[]{:S(2)}) collective-permute-start(bf16[32,512]{1,0:T(8,128)(2,1)S(1)} %get-tuple-element.642), channel_id=1, source_target_pairs={{0,32},{16,48},{32,0},{48,16},{64,96},{80,112},{96,64},{112,80},{1... | collective-permute-start | bytes 98312 | tf_op jit(solution)/shard_map/ppermute | solution.py:29
  614.2 6.8 %collective-permute-start.2 = (bf16[32,512]{1,0:T(8,128)(2,1)S(1)}, bf16[32,512]{1,0:T(8,128)(2,1)S(1)}, u32[]{:S(2)}, u32[]{:S(2)}) collective-permute-start(bf16[32,512]{1,0:T(8,128)(2,1)S(1)} %get-tuple-element.641), channel_id=1, source_target_pairs={{0,48},{16,32},{32,16},{48,0},{64,112},{80,96},{96,80},{112,64},{1... | collective-permute-start | bytes 98312 | tf_op jit(solution)/shard_map/ppermute | solution.py:29
  614.8 6.2 collective-permute-start.3
  617.4 5.0 collective-permute-start.4
  618.1 5.2 collective-permute-start.5
  620.4 4.8 collective-permute-start.6
  657.2 13.2 %all-to-all-start.2 = ((bf16[8,32,512]{2,1,0:T(8,128)(2,1)}), bf16[8,32,512]{2,1,0:T(8,128)(2,1)S(1)}, u32[]{:S(2)}, u32[]{:S(2)}) async-start(bf16[8,32,512]{2,1,0:T(8,128)(2,1)} %bitcast.291), calls=%async_computation.3 | async-start | bytes 524288 | tf_op jit(solution)/shard_map/all_to_all | solution.py:151
Sparse Core Ops, SparseCore 0:
  21.3 52.2 all-gather.1
  500.3 156.7 reduce-scatter.1
